TPU v7x, 512 devices: a whole 4x4x16 slice. The times are simulated.
512 devices in a mesh: node: 64 (over y, z), local: 8 (over x, core).
Axes of the slice: x: 4, y: 4, z: 16, core: 2. Of those that a mesh axis runs over, the one named last changes fastest.
Arguments:
- grad_out: bfloat16 [65536, 3584], P(('node', 'local')), may hold values from -6 to 6
- expert_ids: int32 [65536, 8], P(('node', 'local')), may hold values from 0 to 255, as said below
- gate_weights: float32 [65536, 8], P(('node', 'local')), may hold values from 0.05 to 0.35
- saved_hidden: bfloat16 [64, 1024, 1024], P('node', None, 'local'), may hold values from -0.59765625 to 0.59765625
- down_weight: bfloat16 [64, 1024, 3584], P('node', 'local'), may hold values from -0.1875 to 0.1875
- second_moment: bfloat16 [64, 1024, 3584], P('node', 'local'), may hold values from 0.0019989014 to 0.25
Outputs:
- gate_weight_gradient: float32 [65536, 8], P(('node', 'local'))
- hidden_grad: bfloat16 [64, 1024, 1024], P('node', None, 'local')
- new_weight: bfloat16 [64, 1024, 3584], P('node', 'local')
- new_second: bfloat16 [64, 1024, 3584], P('node', 'local')
Inputs may be any that keep to these rules, and one draw needn't show every extreme that they name: `expert_ids`: each row names 8 different experts on at most 4 nodes (node = id // 4), two on each; at most one per row is in flight (id % 4 == 0). Among the rows of one device at most 2 name the in-flight expert of any one node, and in every draw some node receives exactly 2 from every device.
All inputs are finite; a program needn't handle non-finite values.
Results may differ from a plain program's by a relative error of at most 0.0051.
Values may be sent and summed in bfloat16 or wider, within the bound.
No kernel may reach another device: no remote copies, remote signals or barrier semaphores. Data moves between devices by JAX's collectives and lax.ppermute only.
A program may use at most 128 MiB of HBM per device.

v0:
```python
import jax
import jax.numpy as jnp
from jax import lax
from jax.sharding import PartitionSpec as P

EXPERTS_PER_HOST = 4
CAP = 2
beta_second = 0.95
learn_rate = 0.002
decay_rate = 0.1
epsilon = 1e-08
correct_second = 0.994079470779666


def route(picked_experts, gate_values, node_count):
    transit_rows = picked_experts % EXPERTS_PER_HOST == 0
    row_present = jnp.any(transit_rows, 1)
    destination_node = jnp.sum(jnp.where(transit_rows, picked_experts // EXPERTS_PER_HOST, 0), 1)
    tokens = picked_experts.shape[0]
    same = (
        (destination_node[:, None] == destination_node[None, :])
        & row_present[None, :]
        & (jnp.arange(tokens)[None, :] < jnp.arange(tokens)[:, None])
    )
    within_rank = jnp.sum(same.astype(jnp.int32), 1)
    slot_index = destination_node * CAP + within_rank
    expert_location = (
        jnp.arange(node_count * CAP, dtype=jnp.int32)[:, None] == slot_index[None, :]
    ) & row_present[None, :]
    matched_gate = jnp.sum(jnp.where(transit_rows, gate_values, 0.0), 1).astype(jnp.bfloat16)
    return (expert_location, transit_rows, row_present, matched_gate.astype(jnp.float32))


def on_device(grad_out, expert_ids, gate_weights, saved_hidden, down_weight, second_moment):
    node_count = lax.axis_size("node")
    members = lax.axis_size("local")
    feature_count = grad_out.shape[1]
    expert_location, transit_rows, row_present, gate = route(expert_ids, gate_weights, node_count)
    slot_gate = jnp.sum(jnp.where(expert_location, gate[None, :], 0.0), 1)
    picked = jnp.dot(
        expert_location.astype(jnp.bfloat16), grad_out, preferred_element_type=jnp.float32
    )
    scaled_out = (slot_gate[:, None] * picked).astype(jnp.bfloat16)
    arrived = lax.all_to_all(
        scaled_out.reshape(node_count, CAP, feature_count),
        "node",
        split_axis=0,
        concat_axis=0,
        tiled=True,
    )
    scaled = lax.all_gather(
        arrived.reshape(node_count * CAP, feature_count), "local", axis=0, tiled=True
    )
    weight_now = down_weight[0]
    hidden_now = saved_hidden[0]
    hidden_f = lax.dot_general(
        scaled, weight_now, (((1,), (1,)), ((), ())), preferred_element_type=jnp.float32
    )
    slot_score = jnp.sum(hidden_f * hidden_now.astype(jnp.float32), 1)
    grad = lax.dot_general(
        hidden_now, scaled, (((0,), (0,)), ((), ())), preferred_element_type=jnp.float32
    )
    second_new = (
        beta_second * second_moment[0].astype(jnp.float32) + (1.0 - beta_second) * grad * grad
    )
    weight_f = weight_now.astype(jnp.float32)
    update = grad / (jnp.sqrt(second_new / correct_second) + epsilon) + decay_rate * weight_f
    weight_new = weight_f - learn_rate * update
    score_terms = slot_score.reshape(members, node_count * CAP)
    summed = lax.psum(score_terms, "local")
    own_terms = lax.dynamic_slice_in_dim(summed, lax.axis_index("local"), 1, 0)
    returned = lax.all_to_all(
        own_terms.reshape(node_count, CAP), "node", split_axis=0, concat_axis=0, tiled=True
    )
    returned_flat = returned.reshape(node_count * CAP)
    token_score = jnp.sum(jnp.where(expert_location, returned_flat[:, None], 0.0), 0)
    token_gradient = jnp.where(row_present, token_score / jnp.where(row_present, gate, 1.0), 0.0)
    gate_weight_gradient = jnp.where(transit_rows, token_gradient[:, None], 0.0)
    return (
        gate_weight_gradient,
        hidden_f.astype(jnp.bfloat16)[None],
        weight_new.astype(jnp.bfloat16)[None],
        second_new.astype(jnp.bfloat16)[None],
    )


def solution(mesh):
    return jax.shard_map(
        on_device,
        mesh=mesh,
        in_specs=(
            P(("node", "local"), None),
            P(("node", "local"), None),
            P(("node", "local"), None),
            P("node", None, "local"),
            P("node", "local", None),
            P("node", "local", None),
        ),
        out_specs=(
            P(("node", "local"), None),
            P("node", None, "local"),
            P("node", "local", None),
            P("node", "local", None),
        ),
        check_vma=False,
    )
```

profile of v0, /device:TPU:8, one launch (start us, length us, event | category | flops | bytes accessed | tf_op | source)
XLA Modules:
  0.0 181.2 jit_solution(6624401985966689629)
XLA Ops:
  7.2 0.0 copy-start
  7.2 0.0 all-gather.2.cloned.1.call-start
  7.2 0.8 fusion.18
  8.0 0.7 select_reduce_fusion.2
  8.7 0.0 copy-start.5
  8.7 0.2 convert_reduce_fusion
  8.9 0.1 select_reduce_fusion.1
  9.0 0.3 copy-done.5
  9.3 0.0 copy-done
  9.3 0.4 fusion
  9.7 0.3 reshape.51
  10.1 66.9 %all_to_all.14 = bf16[64,2,3584]{2,1,0:T(2,128)(2,1)S(1)} all-to-all(bf16[64,2,3584]{2,1,0:T(2,128)(2,1)S(1)} %reshape.51), channel_id=1, replica_groups=mesh['node'=64,'local'=8] {'node'}, dimensions={0} | all-to-all | bytes 1835008 | tf_op jit(solution)/shard_map/all_to_all | solution.py:44
  77.0 0.0 copy-start.4
  77.0 0.0 copy-start.1
  77.0 1.3 reshape.52
  78.3 0.0 copy-start.2
  78.3 0.0 all-gather.2.cloned.1.call-update
  78.3 0.0 copy-done.4
  78.3 0.1 copy.30
  78.5 0.0 copy-done.1
  78.5 1.3 copy.32
  79.7 0.0 copy-done.2
  79.7 1.3 copy.29
  81.0 0.0 copy-start.3
  81.0 42.7 %all-gather.2.cloned.1.call-done = bf16[1024,3584]{1,0:T(8,128)(2,1)} async-done(((bf16[128,3584]{1,0:T(8,128)(2,1)}), bf16[1024,3584]{1,0:T(8,128)(2,1)}) %all-gather.2.cloned.1.call-update) | async-done | bytes 7340048 | tf_op jit(solution)/shard_map/all_gather | solution.py:51
  123.7 5.5 %convert_bitcast_fusion = (bf16[1,1024,128]{1,2,0:T(8,128)(2,1)S(1)}, f32[1024]{0:T(1024)S(1)}) fusion(bf16[1,1024,128]{1,2,0:T(8,128)(2,1)S(1)} %copy.30, bf16[1024,3584]{1,0:T(8,128)(2,1)} %all-gather.2.cloned.1.call-done, bf16[1,128,3584]{2,1,0:T(8,128)(2,1)S(1)} %copy-done.2), kind=kOutput, calls=%fused_computation.17 | convolution fusion | flops 940047360 | bytes 8785920 | tf_op jit(solution)/shard_map/dot_general | solution.py:56
  129.2 13.2 %psum.7 = f32[8,128]{1,0:T(8,128)S(1)} all-reduce(f32[8,128]{1,0:T(8,128)S(1)} %bitcast.41), channel_id=1, replica_groups=mesh['node'=64,'local'=8] {'local'}, use_global_device_ids=true, to_apply=%region_6.7 | all-reduce | flops 1024 | bytes 8192 | tf_op jit(solution)/shard_map/psum | solution.py:70
  142.4 0.7 all_to_all.10
  143.2 15.8 %all-to-all-start.1 = ((f32[64,1,2]{2,1,0:T(1,128)}), f32[64,1,2]{2,1,0:T(1,128)S(1)}, u32[]{:S(2)}, u32[]{:S(2)}) async-start(f32[64,1,2]{2,1,0:T(1,128)} %bitcast.3), calls=%async_computation.1 | async-start | bytes 65536 | tf_op jit(solution)/shard_map/all_to_all | solution.py:72
  158.9 0.0 copy-done.3
  158.9 7.2 %fusion.6 = (bf16[1,128,3584]{1,2,0:T(8,128)(2,1)}, bf16[1,128,3584]{1,2,0:T(8,128)(2,1)S(1)}) fusion(bf16[1,128,3584]{1,2,0:T(8,128)(2,1)S(1)} %copy-done.3, bf16[1,128,3584]{1,2,0:T(8,128)(2,1)} %copy.29, bf16[1024,3584]{1,0:T(8,128)(2,1)} %all-gather.2.cloned.1.call-done, bf16[1,1024,128]{2,1,0:T(8,128)(2,1)S(1)} %copy-done.4), kind=kOutput, calls=%fused_computation.11 | convolution fusion | flops 946405376 | bytes 11272192 | tf_op jit(solution)/shard_map/dot_general | solution.py:60
  166.1 0.8 copy.33
  167.0 0.0 copy-start.6
  167.0 2.2 %copy.35 = bf16[1,128,3584]{2,1,0:T(8,128)(2,1)} copy(bf16[1,128,3584]{1,2,0:T(8,128)(2,1)} %get-tuple-element.22) | data formatting | bytes 1835008
  169.2 1.3 copy.34
  170.5 1.8 %all-to-all-done.1 = f32[64,1,2]{2,1,0:T(1,128)S(1)} async-done(((f32[64,1,2]{2,1,0:T(1,128)}), f32[64,1,2]{2,1,0:T(1,128)S(1)}, u32[]{:S(2)}, u32[]{:S(2)}) %all-to-all-start.1) | async-done | bytes 544 | tf_op jit(solution)/shard_map/all_to_all | solution.py:72
  172.3 0.5 broadcast.39
  172.8 0.7 reduce.7
  173.5 0.1 broadcast_in_dim.70
  173.7 0.1 select_reduce_fusion
  173.8 0.0 copy-done.6
  173.8 0.6 broadcast_select_fusion
  (5 shorter events, 0.1 us)
Async XLA Ops:
  7.2 2.1 %copy-start = (bf16[128,3584]{1,0:T(8,128)(2,1)S(1)}, bf16[128,3584]{1,0:T(8,128)(2,1)}, u32[]{:S(2)}) copy-start(bf16[128,3584]{1,0:T(8,128)(2,1)} %param.6) | copy-start | bytes 2752516
  7.2 116.5 %all-gather.2.cloned.1.call-start = ((), (), s32[]{:S(2)}) async-start(), calls=%async_computation.2 | async-start | bytes 8257536 | tf_op jit(solution)/shard_map/all_gather | solution.py:51
  8.7 0.6 copy-start.5
  77.0 1.3 copy-start.4
  77.0 1.5 copy-start.1
  78.3 1.5 copy-start.2
  81.0 77.9 %copy-start.3 = (bf16[1,128,3584]{1,2,0:T(8,128)(2,1)S(1)}, bf16[1,128,3584]{1,2,0:T(8,128)(2,1)}, u32[]{:S(2)}) copy-start(bf16[1,128,3584]{1,2,0:T(8,128)(2,1)} %copy.32) | copy-start | bytes 2752516
  143.2 29.1 %all-to-all-start.1 = ((f32[64,1,2]{2,1,0:T(1,128)}), f32[64,1,2]{2,1,0:T(1,128)S(1)}, u32[]{:S(2)}, u32[]{:S(2)}) async-start(f32[64,1,2]{2,1,0:T(1,128)} %bitcast.3), calls=%async_computation.1 | async-start | bytes 65536 | tf_op jit(solution)/shard_map/all_to_all | solution.py:72
  167.0 6.8 %copy-start.6 = (bf16[128]{0:T(256)(128)(2,1)S(1)}, bf16[128]{0:T(256)(128)(2,1)}, u32[]{:S(2)}) copy-start(bf16[128]{0:T(256)(128)(2,1)} %copy-done.5) | copy-start | bytes 772
Sparse Core Ops, SparseCore 0:
  78.4 45.2 all-gather.1
where the time goes:
time: 182 us; the launch traced here: 181 us
  blocking collectives  80.1 us (44%)
  waiting for transfers between devices  44.5 us (24%)
  starting transfers between devices  15.8 us (9%)
  between operations  14.2 us (8%)
  matrix products  13.1 us (7%)
  local copies, waits for them, and re-layouts  10.3 us (6%)
  other arithmetic  3.23 us (2%)
    all_to_all x1, blocking collectives, on_device(): lax.all_to_all(scaled_out.reshape(node_count, CAP, feature_count), 'node'...  66.9 us
    all_gather x1, waiting for transfers between devices, on_device(): lax.all_gather(arrived.reshape(node_count * CAP, feature_count), 'local',...  42.7 us
    all_to_all x1, starting transfers between devices, on_device(): lax.all_to_all(own_terms.reshape(node_count, CAP), 'node', split_axis=0,...  15.8 us
    psum x1, blocking collectives, on_device(): summed = lax.psum(score_terms, 'local')  13.2 us
    unnamed x20, local copies, waits for them, and re-layouts  7.28 us
    dot_general x1, matrix products, on_device(): lax.dot_general(hidden_now, scaled, (((0,), (0,)), ((), ())), preferred_e...  7.21 us
    dot_general x1, matrix products, on_device(): lax.dot_general(scaled, weight_now, (((1,), (1,)), ((), ())), preferred_e...  5.51 us
  transfers between devices with their start and end apart: 2, of which 2 were waited for; matrix products, arithmetic and copies ran while one was open for 8% of the time, Pallas kernels for 0%

commit v1 on v0

--- a/solution.py
+++ b/solution.py
@@ -10,6 +10,22 @@
 decay_rate = 0.1
 epsilon = 1e-08
 correct_second = 0.994079470779666
+
+
+def collect(x, axis, dim):
+    ways, here, lap = (lax.axis_size(axis), lax.axis_index(axis), x.shape[dim])
+    lengths = [n * ways if d == dim else n for d, n in enumerate(x.shape)]
+    full = lax.dynamic_update_slice_in_dim(jnp.zeros(lengths, x.dtype), x, here * lap, axis=dim)
+    going_up = going_down = x
+    for far in range(1, ways // 2 + 1):
+        going_up = lax.ppermute(going_up, axis, [(d, (d + 1) % ways) for d in range(ways)])
+        full = lax.dynamic_update_slice_in_dim(full, going_up, (here - far) % ways * lap, axis=dim)
+        if 2 * far < ways:
+            going_down = lax.ppermute(going_down, axis, [(d, (d - 1) % ways) for d in range(ways)])
+            full = lax.dynamic_update_slice_in_dim(
+                full, going_down, (here + far) % ways * lap, axis=dim
+            )
+    return full
 
 
 def route(picked_experts, gate_values, node_count):
@@ -48,9 +64,7 @@
         concat_axis=0,
         tiled=True,
     )
-    scaled = lax.all_gather(
-        arrived.reshape(node_count * CAP, feature_count), "local", axis=0, tiled=True
-    )
+    scaled = collect(arrived.reshape(node_count * CAP, feature_count), "local", 0)
     weight_now = down_weight[0]
     hidden_now = saved_hidden[0]
     hidden_f = lax.dot_general(

time: 182 us -> 169 us (0.929)
  the two profiles are of different devices: /device:TPU:8 before, /device:TPU:1 now
where the time goes in v1:
time: 169 us; the launch traced here: 168 us
  blocking collectives  82.6 us (49%)
  waiting for transfers between devices  33.6 us (20%)
  starting transfers between devices  19.9 us (12%)
  local copies, waits for them, and re-layouts  17.7 us (10%)
  matrix products  10.1 us (6%)
  other arithmetic  3.25 us (2%)
    all_to_all x1, blocking collectives, on_device(): lax.all_to_all(scaled_out.reshape(node_count, CAP, feature_count), 'node'...  64.6 us
    ppermute x4, waiting for transfers between devices, collect(): lax.ppermute(going_up, axis, [(d, (d + 1) % ways) for d in range(ways)])  32.3 us
    psum x1, blocking collectives, on_device(): summed = lax.psum(score_terms, 'local')  18 us
    ppermute x4, starting transfers between devices, collect(): lax.ppermute(going_up, axis, [(d, (d + 1) % ways) for d in range(ways)])  12.5 us
    unnamed x20, local copies, waits for them, and re-layouts  12.2 us
    dot_general x1, matrix products, on_device(): lax.dot_general(hidden_now, scaled, (((0,), (0,)), ((), ())), preferred_e...  7.32 us
    all_to_all x1, starting transfers between devices, on_device(): lax.all_to_all(own_terms.reshape(node_count, CAP), 'node', split_axis=0,...  6.25 us
  transfers between devices with their start and end apart: 8, of which 7 were waited for; matrix products, arithmetic and copies ran while one was open for 12% of the time, Pallas kernels for 0%

profile of v1, /device:TPU:1, one launch (start us, length us, event | category | flops | bytes accessed | tf_op | source)
XLA Modules:
  0.0 168.1 jit_solution(9749196867345817361)
XLA Ops:
  0.6 0.0 copy-start
  0.7 0.8 fusion.18
  1.5 0.2 convert_reduce_fusion
  1.7 0.7 select_reduce_fusion.2
  2.4 0.1 select_reduce_fusion.1
  2.5 0.4 fusion
  2.9 0.3 reshape.51
  3.3 64.6 %all_to_all.14 = bf16[64,2,3584]{2,1,0:T(2,128)(2,1)S(1)} all-to-all(bf16[64,2,3584]{2,1,0:T(2,128)(2,1)S(1)} %reshape.51), channel_id=1, replica_groups=mesh['node'=64,'local'=8] {'node'}, dimensions={0} | all-to-all | bytes 1835008 | tf_op jit(solution)/shard_map/all_to_all | solution.py:60
  67.8 0.3 reshape.52
  68.2 5.1 %collective-permute-start = (bf16[128,3584]{1,0:T(8,128)(2,1)S(1)}, bf16[128,3584]{1,0:T(8,128)(2,1)}, u32[]{:S(2)}, u32[]{:S(2)}) collective-permute-start(bf16[128,3584]{1,0:T(8,128)(2,1)S(1)} %reshape.52), channel_id=1, source_target_pairs={{0,1},{1,2},{2,3},{3,4},{4,5},{5,6},{6,7},{7,0},{8,9},{9,10},{10,1... | collective-permute-start | bytes 2752520 | tf_op jit(solution)/shard_map/ppermute | solution.py:21
  73.2 1.5 copy.29
  74.8 2.2 %copy.32 = bf16[1,128,3584]{1,2,0:T(8,128)(2,1)} copy(bf16[1,128,3584]{2,1,0:T(8,128)(2,1)} %param.11) | data formatting | bytes 1835008 | tf_op args[5]
  77.0 0.1 copy.30
  77.2 0.5 broadcast_in_dim.70
  77.7 0.1 constant_dynamic-update-slice_fusion.7
  77.8 5.8 %collective-permute-done = bf16[128,3584]{1,0:T(8,128)(2,1)} collective-permute-done((bf16[128,3584]{1,0:T(8,128)(2,1)S(1)}, bf16[128,3584]{1,0:T(8,128)(2,1)}, u32[]{:S(2)}, u32[]{:S(2)}) %collective-permute-start) | collective-permute-done | bytes 917536 | tf_op jit(solution)/shard_map/ppermute | solution.py:21
  83.6 2.6 %collective-permute-start.2 = (bf16[128,3584]{1,0:T(8,128)(2,1)}, bf16[128,3584]{1,0:T(8,128)(2,1)S(1)}, u32[]{:S(2)}, u32[]{:S(2)}) collective-permute-start(bf16[128,3584]{1,0:T(8,128)(2,1)} %collective-permute-done), channel_id=1, source_target_pairs={{0,1},{1,2},{2,3},{3,4},{4,5},{5,6},{6,7},{7,0},{8,9},{9,10},{10,1... | collective-permute-start | bytes 2752520 | tf_op jit(solution)/shard_map/ppermute | solution.py:21
  86.2 0.1 collective-permute-start.3
  86.3 1.3 constant_dynamic-update-slice_fusion.6
  87.5 1.3 constant_dynamic-update-slice_fusion.5
  88.8 8.0 %collective-permute-done.2 = bf16[128,3584]{1,0:T(8,128)(2,1)S(1)} collective-permute-done((bf16[128,3584]{1,0:T(8,128)(2,1)}, bf16[128,3584]{1,0:T(8,128)(2,1)S(1)}, u32[]{:S(2)}, u32[]{:S(2)}) %collective-permute-start.2) | collective-permute-done | bytes 917536 | tf_op jit(solution)/shard_map/ppermute | solution.py:21
  96.8 2.4 %collective-permute-start.4 = (bf16[128,3584]{1,0:T(8,128)(2,1)S(1)}, bf16[128,3584]{1,0:T(8,128)(2,1)S(1)}, u32[]{:S(2)}, u32[]{:S(2)}) collective-permute-start(bf16[128,3584]{1,0:T(8,128)(2,1)S(1)} %collective-permute-done.2), channel_id=1, source_target_pairs={{0,1},{1,2},{2,3},{3,4},{4,5},{5,6},{6,7},{7,0},{8,9},{9,10},{10,1... | collective-permute-start | bytes 2752520 | tf_op jit(solution)/shard_map/ppermute | solution.py:21
  99.2 0.3 collective-permute-done.3
  99.5 1.0 collective-permute-start.5
  100.5 0.1 constant_dynamic-update-slice_fusion.4
  100.6 0.1 constant_dynamic-update-slice_fusion.3
  100.7 8.8 %collective-permute-done.4 = bf16[128,3584]{1,0:T(8,128)(2,1)S(1)} collective-permute-done((bf16[128,3584]{1,0:T(8,128)(2,1)S(1)}, bf16[128,3584]{1,0:T(8,128)(2,1)S(1)}, u32[]{:S(2)}, u32[]{:S(2)}) %collective-permute-start.4) | collective-permute-done | bytes 917536 | tf_op jit(solution)/shard_map/ppermute | solution.py:21
  109.5 2.5 %collective-permute-start.6 = (bf16[128,3584]{1,0:T(8,128)(2,1)S(1)}, bf16[128,3584]{1,0:T(8,128)(2,1)S(1)}, u32[]{:S(2)}, u32[]{:S(2)}) collective-permute-start(bf16[128,3584]{1,0:T(8,128)(2,1)S(1)} %collective-permute-done.4), channel_id=1, source_target_pairs={{0,1},{1,2},{2,3},{3,4},{4,5},{5,6},{6,7},{7,0},{8,9},{9,10},{10,1... | collective-permute-start | bytes 2752520 | tf_op jit(solution)/shard_map/ppermute | solution.py:21
  112.0 0.1 constant_dynamic-update-slice_fusion.2
  112.1 0.5 collective-permute-done.5
  112.6 0.1 constant_dynamic-update-slice_fusion.1
  112.7 9.7 %collective-permute-done.6 = bf16[128,3584]{1,0:T(8,128)(2,1)S(1)} collective-permute-done((bf16[128,3584]{1,0:T(8,128)(2,1)S(1)}, bf16[128,3584]{1,0:T(8,128)(2,1)S(1)}, u32[]{:S(2)}, u32[]{:S(2)}) %collective-permute-start.6) | collective-permute-done | bytes 917536 | tf_op jit(solution)/shard_map/ppermute | solution.py:21
  122.3 0.1 constant_dynamic-update-slice_fusion
  122.4 3.0 %copy-done.1 = bf16[1024,3584]{1,0:T(8,128)(2,1)} copy-done((bf16[1024,3584]{1,0:T(8,128)(2,1)}, bf16[1024,3584]{1,0:T(8,128)(2,1)S(1)}, u32[]{:S(2)}) %copy-start.1) | copy-done | bytes 7340056
  125.4 2.4 %convert_bitcast_fusion = (bf16[1,1024,128]{1,2,0:T(8,128)(2,1)S(1)}, f32[1024]{0:T(1024)S(1)}) fusion(bf16[1,1024,128]{1,2,0:T(8,128)(2,1)S(1)} %copy.30, bf16[1024,3584]{1,0:T(8,128)(2,1)S(1)} %constant_dynamic-update-slice_fusion, bf16[1,128,3584]{2,1,0:T(8,128)(2,1)S(1)} %copy-done.2), kind=kOutput, calls=%fused_computation.17 | convolution fusion | flops 940047360 | bytes 8785920 | tf_op jit(solution)/shard_map/dot_general | solution.py:70
  127.8 18.0 %psum.7 = f32[8,128]{1,0:T(8,128)S(1)} all-reduce(f32[8,128]{1,0:T(8,128)S(1)} %bitcast.41), channel_id=1, replica_groups=mesh['node'=64,'local'=8] {'local'}, use_global_device_ids=true, to_apply=%region_6.7 | all-reduce | flops 1024 | bytes 8192 | tf_op jit(solution)/shard_map/psum | solution.py:84
  145.9 0.7 all_to_all.10
  146.6 6.2 %all-to-all-start.1 = ((f32[64,1,2]{2,1,0:T(1,128)}), f32[64,1,2]{2,1,0:T(1,128)S(1)}, u32[]{:S(2)}, u32[]{:S(2)}) async-start(f32[64,1,2]{2,1,0:T(1,128)} %bitcast.3), calls=%async_computation.1 | async-start | bytes 65536 | tf_op jit(solution)/shard_map/all_to_all | solution.py:86
  152.9 7.3 %fusion.6 = (bf16[1,128,3584]{1,2,0:T(8,128)(2,1)}, bf16[1,128,3584]{1,2,0:T(8,128)(2,1)}) fusion(bf16[1,128,3584]{1,2,0:T(8,128)(2,1)S(1)} %copy-done.3, bf16[1,128,3584]{1,2,0:T(8,128)(2,1)S(1)} %copy.29, bf16[1024,3584]{1,0:T(8,128)(2,1)} %copy-done.1, bf16[1,1024,128]{2,1,0:T(8,128)(2,1)S(1)} %copy-done.4), kind=kOutput, calls=%fused_computation.11 | convolution fusion | flops 946405376 | bytes 11272192 | tf_op jit(solution)/shard_map/dot_general | solution.py:74
  160.2 2.2 %copy.34 = bf16[1,128,3584]{2,1,0:T(8,128)(2,1)} copy(bf16[1,128,3584]{1,2,0:T(8,128)(2,1)} %get-tuple-element.23) | data formatting | bytes 1835008
  162.4 2.2 %copy.35 = bf16[1,128,3584]{2,1,0:T(8,128)(2,1)} copy(bf16[1,128,3584]{1,2,0:T(8,128)(2,1)} %get-tuple-element.22) | data formatting | bytes 1835008
  164.6 0.8 copy.33
  165.5 0.5 all-to-all-done.1
  166.0 0.5 broadcast.50
  166.5 0.7 reduce.7
  167.2 0.1 broadcast_in_dim.74
  167.4 0.1 select_reduce_fusion
  167.5 0.6 broadcast_select_fusion
  (19 shorter events, 0.1 us)
Async XLA Ops:
  0.6 1.9 %copy-start = (bf16[128,3584]{1,0:T(8,128)(2,1)S(1)}, bf16[128,3584]{1,0:T(8,128)(2,1)}, u32[]{:S(2)}) copy-start(bf16[128,3584]{1,0:T(8,128)(2,1)} %param.6) | copy-start | bytes 2752516
  0.6 76.4 %copy-start.4 = (bf16[1,1024,128]{2,1,0:T(8,128)(2,1)S(1)}, bf16[1,1024,128]{2,1,0:T(8,128)(2,1)}, u32[]{:S(2)}) copy-start(bf16[1,1024,128]{2,1,0:T(8,128)(2,1)} %param.9) | copy-start | bytes 786436
  2.4 72.4 %copy-start.5 = (bf16[128]{0:T(256)(128)(2,1)}, bf16[128]{0:T(256)(128)(2,1)S(1)}, u32[]{:S(2)}) copy-start(bf16[128]{0:T(256)(128)(2,1)S(1)} %select_reduce_fusion.2) | copy-start | bytes 772
  68.2 15.4 %collective-permute-start = (bf16[128,3584]{1,0:T(8,128)(2,1)S(1)}, bf16[128,3584]{1,0:T(8,128)(2,1)}, u32[]{:S(2)}, u32[]{:S(2)}) collective-permute-start(bf16[128,3584]{1,0:T(8,128)(2,1)S(1)} %reshape.52), channel_id=1, source_target_pairs={{0,1},{1,2},{2,3},{3,4},{4,5},{5,6},{6,7},{7,0},{8,9},{9,10},{10,1... | collective-permute-start | bytes 2752520 | tf_op jit(solution)/shard_map/ppermute | solution.py:21
  73.2 12.9 %collective-permute-start.1 = (bf16[128,3584]{1,0:T(8,128)(2,1)S(1)}, bf16[128,3584]{1,0:T(8,128)(2,1)}, u32[]{:S(2)}, u32[]{:S(2)}) collective-permute-start(bf16[128,3584]{1,0:T(8,128)(2,1)S(1)} %reshape.52), channel_id=1, source_target_pairs={{0,7},{1,0},{2,1},{3,2},{4,3},{5,4},{6,5},{7,6},{8,15},{9,8},{10,9... | collective-permute-start | bytes 2752520 | tf_op jit(solution)/shard_map/ppermute | solution.py:24
  77.7 47.7 %copy-start.2 = (bf16[1,128,3584]{2,1,0:T(8,128)(2,1)S(1)}, bf16[1,128,3584]{2,1,0:T(8,128)(2,1)}, u32[]{:S(2)}) copy-start(bf16[1,128,3584]{2,1,0:T(8,128)(2,1)} %param.10) | copy-start | bytes 2752516
  83.6 13.2 %collective-permute-start.2 = (bf16[128,3584]{1,0:T(8,128)(2,1)}, bf16[128,3584]{1,0:T(8,128)(2,1)S(1)}, u32[]{:S(2)}, u32[]{:S(2)}) collective-permute-start(bf16[128,3584]{1,0:T(8,128)(2,1)} %collective-permute-done), channel_id=1, source_target_pairs={{0,1},{1,2},{2,3},{3,4},{4,5},{5,6},{6,7},{7,0},{8,9},{9,10},{10,1... | collective-permute-start | bytes 2752520 | tf_op jit(solution)/shard_map/ppermute | solution.py:21
  86.2 13.3 %collective-permute-start.3 = (bf16[128,3584]{1,0:T(8,128)(2,1)}, bf16[128,3584]{1,0:T(8,128)(2,1)S(1)}, u32[]{:S(2)}, u32[]{:S(2)}) collective-permute-start(bf16[128,3584]{1,0:T(8,128)(2,1)} %collective-permute-done.1), channel_id=1, source_target_pairs={{0,7},{1,0},{2,1},{3,2},{4,3},{5,4},{6,5},{7,6},{8,15},{9,8},{10,9... | collective-permute-start | bytes 2752520 | tf_op jit(solution)/shard_map/ppermute | solution.py:24
  96.8 12.7 %collective-permute-start.4 = (bf16[128,3584]{1,0:T(8,128)(2,1)S(1)}, bf16[128,3584]{1,0:T(8,128)(2,1)S(1)}, u32[]{:S(2)}, u32[]{:S(2)}) collective-permute-start(bf16[128,3584]{1,0:T(8,128)(2,1)S(1)} %collective-permute-done.2), channel_id=1, source_target_pairs={{0,1},{1,2},{2,3},{3,4},{4,5},{5,6},{6,7},{7,0},{8,9},{9,10},{10,1... | collective-permute-start | bytes 2752520 | tf_op jit(solution)/shard_map/ppermute | solution.py:21
  99.5 13.1 %collective-permute-start.5 = (bf16[128,3584]{1,0:T(8,128)(2,1)S(1)}, bf16[128,3584]{1,0:T(8,128)(2,1)S(1)}, u32[]{:S(2)}, u32[]{:S(2)}) collective-permute-start(bf16[128,3584]{1,0:T(8,128)(2,1)S(1)} %collective-permute-done.3), channel_id=1, source_target_pairs={{0,7},{1,0},{2,1},{3,2},{4,3},{5,4},{6,5},{7,6},{8,15},{9,8},{10,9... | collective-permute-start | bytes 2752520 | tf_op jit(solution)/shard_map/ppermute | solution.py:24
  109.5 12.8 %collective-permute-start.6 = (bf16[128,3584]{1,0:T(8,128)(2,1)S(1)}, bf16[128,3584]{1,0:T(8,128)(2,1)S(1)}, u32[]{:S(2)}, u32[]{:S(2)}) collective-permute-start(bf16[128,3584]{1,0:T(8,128)(2,1)S(1)} %collective-permute-done.4), channel_id=1, source_target_pairs={{0,1},{1,2},{2,3},{3,4},{4,5},{5,6},{6,7},{7,0},{8,9},{9,10},{10,1... | collective-permute-start | bytes 2752520 | tf_op jit(solution)/shard_map/ppermute | solution.py:21
  112.1 40.8 %copy-start.3 = (bf16[1,128,3584]{1,2,0:T(8,128)(2,1)S(1)}, bf16[1,128,3584]{1,2,0:T(8,128)(2,1)}, u32[]{:S(2)}) copy-start(bf16[1,128,3584]{1,2,0:T(8,128)(2,1)} %copy.32) | copy-start | bytes 2752516
  122.4 3.0 %copy-start.1 = (bf16[1024,3584]{1,0:T(8,128)(2,1)}, bf16[1024,3584]{1,0:T(8,128)(2,1)S(1)}, u32[]{:S(2)}) copy-start(bf16[1024,3584]{1,0:T(8,128)(2,1)S(1)} %constant_dynamic-update-slice_fusion) | copy-start | bytes 22020100
  146.6 19.4 %all-to-all-start.1 = ((f32[64,1,2]{2,1,0:T(1,128)}), f32[64,1,2]{2,1,0:T(1,128)S(1)}, u32[]{:S(2)}, u32[]{:S(2)}) async-start(f32[64,1,2]{2,1,0:T(1,128)} %bitcast.3), calls=%async_computation.1 | async-start | bytes 65536 | tf_op jit(solution)/shard_map/all_to_all | solution.py:86
  152.9 14.6 %copy-start.6 = (bf16[128]{0:T(256)(128)(2,1)S(1)}, bf16[128]{0:T(256)(128)(2,1)}, u32[]{:S(2)}) copy-start(bf16[128]{0:T(256)(128)(2,1)} %copy-done.5) | copy-start | bytes 772
